TPU v7x, 512 devices: a whole 4x8x8 slice. The times are simulated.
512 devices in a mesh: expert: 32 (over y_lo, z, core), dp: 16 (over y_hi, x).
Axes of the slice: x: 4, y: 8 (y_hi: 4, y_lo: 2; y = y_hi * 2 + y_lo), z: 8, core: 2. Of those that a mesh axis runs over, the one named last changes fastest.
Arguments:
- tokens: bfloat16 [65536, 3584], P(('expert', 'dp')), may hold values from -6 to 6
- expert_ids: int32 [65536, 8], P(('expert', 'dp')), may hold values from 0 to 255, all different within a row
- gate_probs: float32 [65536, 8], P(('expert', 'dp')), may hold values from 0.02 to 0.5
- out_grad: bfloat16 [65536, 3584], P(('expert', 'dp')), may hold values from -6 to 6
- w_gate: bfloat16 [32, 1024, 3584], P('expert', 'dp'), may hold values from -0.09375 to 0.09375
- w_up: bfloat16 [32, 1024, 3584], P('expert', 'dp'), may hold values from -0.09375 to 0.09375
- w_down: bfloat16 [32, 1024, 3584], P('expert', 'dp'), may hold values from -0.1875 to 0.1875
Outputs:
- grad_gate: bfloat16 [32, 1024, 3584], P('expert', 'dp')
- grad_up: bfloat16 [32, 1024, 3584], P('expert', 'dp')
- grad_down: bfloat16 [32, 1024, 3584], P('expert', 'dp')
All inputs are finite; a program needn't handle non-finite values.
Results may differ from a plain program's by a relative error of at most 0.0058.
Values may be sent and summed in bfloat16 or wider, within the bound.
A program may use at most 64 MiB of HBM per device.

v0:
```python
import jax
import jax.numpy as jnp
from jax import lax
from jax.sharding import PartitionSpec as P

CAP = 2


def local_factors(rows_x, rows_dy, weight_gate, weight_up, weight_down):
    contract = (((1,), (1,)), ((), ()))
    gate_pre = lax.dot_general(rows_x, weight_gate, contract, preferred_element_type=jnp.float32)
    up_pre = lax.dot_general(rows_x, weight_up, contract, preferred_element_type=jnp.float32)
    back_grad = lax.dot_general(rows_dy, weight_down, contract, preferred_element_type=jnp.float32)
    sig_gate = jax.nn.sigmoid(gate_pre)
    act_gate = gate_pre * sig_gate
    hidden = (act_gate * up_pre).astype(jnp.bfloat16)
    d_gate = (back_grad * up_pre * sig_gate * (1.0 + gate_pre * (1.0 - sig_gate))).astype(
        jnp.bfloat16
    )
    d_up = (back_grad * act_gate).astype(jnp.bfloat16)
    return (d_gate, d_up, hidden)


def outer_sum(factor, rows):
    return lax.dot_general(
        factor, rows, (((0,), (0,)), ((), ())), preferred_element_type=jnp.float32
    )


def local(tokens, expert_ids, gate_probs, out_grad, w_gate, w_up, w_down):
    n_expert = lax.axis_size("expert")
    experts_all = w_gate.shape[0] * n_expert
    tok_rows, top_count = expert_ids.shape
    feature_count = tokens.shape[1]
    flat_ids = expert_ids.reshape(-1)
    expert_range = jnp.arange(experts_all, dtype=jnp.int32)
    onehot = (flat_ids[:, None] == expert_range[None, :]).astype(jnp.int32)
    before = jnp.cumsum(onehot, axis=0) - onehot
    slot_rank = jnp.sum(before * onehot, axis=1)
    kept_mask = (flat_ids < experts_all) & (slot_rank < CAP)
    slot_index = jnp.where(kept_mask, flat_ids * CAP + slot_rank, -1)
    slot_range = jnp.arange(experts_all * CAP, dtype=jnp.int32)
    matches = (slot_index[None, :] == slot_range[:, None]).astype(jnp.float32)
    matches = matches.reshape(experts_all * CAP, tok_rows, top_count)
    picker = jnp.sum(matches, axis=2).astype(jnp.bfloat16)
    slot_prob = jnp.sum(matches * gate_probs[None, :, :], axis=(1, 2))
    sent_x = jnp.dot(picker, tokens, preferred_element_type=jnp.float32).astype(jnp.bfloat16)
    sent_dy = (
        jnp.dot(picker, out_grad, preferred_element_type=jnp.float32) * slot_prob[:, None]
    ).astype(jnp.bfloat16)
    sent_x = sent_x.reshape(experts_all, CAP, feature_count)
    sent_dy = sent_dy.reshape(experts_all, CAP, feature_count)
    recv_x, recv_dy = (
        lax.all_to_all(sent_x, "expert", split_axis=0, concat_axis=0, tiled=True),
        lax.all_to_all(sent_dy, "expert", split_axis=0, concat_axis=0, tiled=True),
    )
    rows_x = recv_x.reshape(-1, feature_count)
    rows_dy = recv_dy.reshape(-1, feature_count)
    piece_x = lax.all_gather(rows_x, "dp", axis=0, tiled=True)
    piece_dy = lax.all_gather(rows_dy, "dp", axis=0, tiled=True)
    d_gate, d_up, hidden = local_factors(piece_x, piece_dy, w_gate[0], w_up[0], w_down[0])
    term_gate = outer_sum(d_gate, piece_x)
    term_up = outer_sum(d_up, piece_x)
    term_down = outer_sum(hidden, piece_dy)
    return (
        term_gate.astype(jnp.bfloat16)[None],
        term_up.astype(jnp.bfloat16)[None],
        term_down.astype(jnp.bfloat16)[None],
    )


def solution(mesh):
    in_specs = (
        P(("expert", "dp"), None),
        P(("expert", "dp"), None),
        P(("expert", "dp"), None),
        P(("expert", "dp"), None),
        P("expert", "dp", None),
        P("expert", "dp", None),
        P("expert", "dp", None),
    )
    out_specs = (P("expert", "dp", None), P("expert", "dp", None), P("expert", "dp", None))
    return jax.shard_map(local, mesh=mesh, in_specs=in_specs, out_specs=out_specs, check_vma=False)
```

profile of v0, /device:TPU:1, one launch (start us, length us, event | category | flops | bytes accessed | tf_op | source)
XLA Modules:
  0.0 293.1 jit_solution(2632505541616493926)
XLA Ops:
  7.2 0.0 copy-start
  7.2 0.0 copy-start.3
  7.2 0.0 all-gather.5.cloned.1.call-start
  7.2 0.9 copy.30
  8.1 0.1 eq.43
  8.2 0.1 eq.39
  8.3 9.0 %reduce-window.6 = s32[32,8,128]{2,1,0:T(8,128)S(1)} reduce-window(s32[32,8,128]{2,1,0:T(8,128)S(1)} %fusion.15, s32[]{:T(128)} %constant.4.clone.1), window={size=1x1x128 pad=0_0x0_0x127_0}, to_apply=%region_0.0 | reduce-window | flops 4161536 | bytes 262148 | tf_op jit(solution)/shard_map/reduce-window
  17.3 0.1 slice.8
  17.4 0.1 copy.32
  17.6 0.1 copy.33
  17.7 0.1 broadcast_add_fusion
  17.8 0.1 reduce_sum.30
  18.0 0.7 add_select_fusion
  18.7 1.2 select_reduce_fusion
  19.9 0.0 copy-done
  19.9 0.3 convolution_convert_fusion.3
  20.2 0.2 reshape.64
  20.4 27.1 %all_to_all.10 = bf16[32,2,3584]{2,1,0:T(2,128)(2,1)S(1)} all-to-all(bf16[32,2,3584]{2,1,0:T(2,128)(2,1)S(1)} %reshape.64), channel_id=1, replica_groups=mesh['expert'=32,'dp'=16] {'expert'}, dimensions={0} | all-to-all | bytes 917504 | tf_op jit(solution)/shard_map/all_to_all | solution.py:54
  47.5 0.0 copy-start.4
  47.5 0.9 reshape.65
  48.4 0.0 all-gather.5.cloned.1.call-update
  48.4 0.0 all-gather.3.cloned.1.call-start
  48.5 1.5 fusion
  49.9 0.2 reshape.62
  50.1 19.5 %all_to_all.11 = bf16[32,2,3584]{2,1,0:T(2,128)(2,1)S(1)} all-to-all(bf16[32,2,3584]{2,1,0:T(2,128)(2,1)S(1)} %reshape.62), channel_id=1, replica_groups=mesh['expert'=32,'dp'=16] {'expert'}, dimensions={0} | all-to-all | bytes 917504 | tf_op jit(solution)/shard_map/all_to_all | solution.py:55
  69.6 0.9 reshape.63
  70.6 0.0 all-gather.3.cloned.1.call-update
  70.6 0.0 copy-start.5
  70.6 85.9 %all-gather.5.cloned.1.call-done = bf16[1024,3584]{1,0:T(8,128)(2,1)} async-done(((bf16[64,3584]{1,0:T(8,128)(2,1)}), bf16[1024,3584]{1,0:T(8,128)(2,1)}) %all-gather.5.cloned.1.call-update) | async-done | bytes 7340048 | tf_op jit(solution)/shard_map/all_gather | solution.py:59
  156.5 0.0 copy-done.3
  156.5 0.0 copy-start.1
  156.5 5.5 %fusion.4 = f32[1024,64]{0,1:T(8,128)S(1)} fusion(bf16[1024,3584]{1,0:T(8,128)(2,1)} %all-gather.5.cloned.1.call-done, bf16[1,64,3584]{2,1,0:T(8,128)(2,1)S(1)} %copy-done.3), kind=kOutput, calls=%fused_computation.9 | convolution fusion | flops 469762048 | bytes 8060928 | tf_op jit(solution)/shard_map/dot_general | solution.py:11
  162.1 0.0 copy-done.4
  162.1 0.0 copy-done.1
  162.1 2.3 fusion.6
  164.4 106.6 %all-gather.3.cloned.1.call-done = bf16[1024,3584]{1,0:T(8,128)(2,1)} async-done(((bf16[64,3584]{1,0:T(8,128)(2,1)}), bf16[1024,3584]{1,0:T(8,128)(2,1)}) %all-gather.3.cloned.1.call-update) | async-done | bytes 7340048 | tf_op jit(solution)/shard_map/all_gather | solution.py:60
  271.0 0.0 copy-done.5
  271.0 0.0 copy-start.2
  271.0 5.5 %fusion.8 = f32[1024,64]{0,1:T(8,128)S(1)} fusion(bf16[1024,3584]{1,0:T(8,128)(2,1)} %all-gather.3.cloned.1.call-done, bf16[1,64,3584]{2,1,0:T(8,128)(2,1)S(1)} %copy-done.5), kind=kOutput, calls=%fused_computation.13 | convolution fusion | flops 469762048 | bytes 8060928 | tf_op jit(solution)/shard_map/dot_general | solution.py:13
  276.6 0.0 copy-done.2
  276.6 0.0 slice-start
  276.6 2.1 fusion.3
  278.7 0.0 slice-start.1
  278.7 5.4 %fusion.1 = bf16[1,64,3584]{2,1,0:T(8,128)(2,1)} fusion(bf16[1024,3584]{1,0:T(8,128)(2,1)} %all-gather.5.cloned.1.call-done, f32[1024,64]{0,1:T(8,128)S(1)} %fusion.4, f32[1024,64]{0,1:T(8,128)S(1)} %fusion.8, f32[1024,64]{0,1:T(8,128)S(1)} %fusion.6), kind=kOutput, calls=%fused_computation.6 | convolution fusion | flops 470646784 | bytes 8585216 | tf_op jit(solution)/shard_map/dot_general | solution.py:25
  284.1 0.0 slice-done
  284.1 0.0 slice-done.1
  284.1 2.1 fusion.2
  (6 shorter events, 0.1 us)
Async XLA Ops:
  7.2 12.8 %copy-start = (bf16[128,3584]{1,0:T(8,128)(2,1)S(1)}, bf16[128,3584]{1,0:T(8,128)(2,1)}, u32[]{:S(2)}) copy-start(bf16[128,3584]{1,0:T(8,128)(2,1)} %param.7) | copy-start | bytes 2752516
  7.2 149.3 %copy-start.3 = (bf16[1,64,3584]{2,1,0:T(8,128)(2,1)S(1)}, bf16[1,64,3584]{2,1,0:T(8,128)(2,1)}, u32[]{:S(2)}) copy-start(bf16[1,64,3584]{2,1,0:T(8,128)(2,1)} %param.11) | copy-start | bytes 1376260
  7.2 149.3 %all-gather.5.cloned.1.call-start = ((), (), s32[]{:S(2)}) async-start(), calls=%async_computation.3 | async-start | bytes 7798784 | tf_op jit(solution)/shard_map/all_gather | solution.py:59
  47.5 114.6 %copy-start.4 = (bf16[1,64,3584]{2,1,0:T(8,128)(2,1)S(1)}, bf16[1,64,3584]{2,1,0:T(8,128)(2,1)}, u32[]{:S(2)}) copy-start(bf16[1,64,3584]{2,1,0:T(8,128)(2,1)} %param.12) | copy-start | bytes 1376260
  48.4 222.6 %all-gather.3.cloned.1.call-start = ((), (), s32[]{:S(2)}) async-start(), calls=%async_computation.2 | async-start | bytes 7798784 | tf_op jit(solution)/shard_map/all_gather | solution.py:60
  70.6 200.4 %copy-start.5 = (bf16[1,64,3584]{2,1,0:T(8,128)(2,1)S(1)}, bf16[1,64,3584]{2,1,0:T(8,128)(2,1)}, u32[]{:S(2)}) copy-start(bf16[1,64,3584]{2,1,0:T(8,128)(2,1)} %param.13) | copy-start | bytes 1376260
  156.5 5.6 %copy-start.1 = (bf16[1024,3584]{1,0:T(8,128)(2,1)S(1)}, bf16[1024,3584]{1,0:T(8,128)(2,1)}, u32[]{:S(2)}) copy-start(bf16[1024,3584]{1,0:T(8,128)(2,1)} %all-gather.5.cloned.1.call-done) | copy-start | bytes 22020100
  271.0 5.5 %copy-start.2 = (bf16[1024,3584]{1,0:T(8,128)(2,1)S(1)}, bf16[1024,3584]{1,0:T(8,128)(2,1)}, u32[]{:S(2)}) copy-start(bf16[1024,3584]{1,0:T(8,128)(2,1)} %all-gather.3.cloned.1.call-done) | copy-start | bytes 22020100
  276.6 7.5 %slice-start = ((s8[7340032]{0:T(1024)(128)(4,1)}), s8[4194304]{0:T(1024)(128)(4,1)S(1)}, s32[]{:S(2)}) async-start(s8[7340032]{0:T(1024)(128)(4,1)} %bitcast.43), calls=%async_computation.4 | async-start | bytes 8388608
  278.7 5.4 %slice-start.1 = ((s8[7340032]{0:T(1024)(128)(4,1)}), s8[3145728]{0:T(1024)(128)(4,1)S(1)}, s32[]{:S(2)}) async-start(s8[7340032]{0:T(1024)(128)(4,1)} %bitcast.43), calls=%async_computation.5 | async-start | bytes 6291456
Sparse Core Ops, SparseCore 0:
  48.6 107.9 all-gather.4
  160.1 110.8 all-gather.2
where the time goes:
time: 293 us
  waiting for transfers between devices  193 us (66%)
  blocking collectives  46.6 us (16%)
  matrix products  24.7 us (8%)
  between operations  14.2 us (5%)
  other arithmetic  11.2 us (4%)
  local copies, waits for them, and re-layouts  3.76 us (1%)
    all_gather x1, waiting for transfers between devices, local(): piece_dy = lax.all_gather(rows_dy, 'dp', axis=0, tiled=True)  107 us
    all_gather x1, waiting for transfers between devices, local(): piece_x = lax.all_gather(rows_x, 'dp', axis=0, tiled=True)  85.9 us
    all_to_all x1, blocking collectives, local(): lax.all_to_all(sent_x, 'expert', split_axis=0, concat_axis=0, tiled=True)  27.1 us
    all_to_all x1, blocking collectives, local(): lax.all_to_all(sent_dy, 'expert', split_axis=0, concat_axis=0, tiled=True)  19.5 us
    dot_general x3, matrix products, outer_sum(): lax.dot_general(factor, rows, (((0,), (0,)), ((), ())), preferred_element...  9.65 us
    another operation x3, other arithmetic  9.15 us
  transfers between devices with their start and end apart: 2, of which 2 were waited for; matrix products, arithmetic and copies ran while one was open for 4% of the time, Pallas kernels for 0%

commit v1 on v0

--- a/solution.py
+++ b/solution.py
@@ -28,6 +28,15 @@
 
 
 def local(tokens, expert_ids, gate_probs, out_grad, w_gate, w_up, w_down):
+
+    def series_all_advance(arr, t0):
+        w1 = jnp.split(
+            lax.all_gather(jnp.concatenate([arr, t0], axis=1), "dp", axis=0, tiled=True),
+            [arr.shape[1]],
+            axis=1,
+        )
+        return w1
+
     n_expert = lax.axis_size("expert")
     experts_all = w_gate.shape[0] * n_expert
     tok_rows, top_count = expert_ids.shape
@@ -56,8 +65,7 @@
     )
     rows_x = recv_x.reshape(-1, feature_count)
     rows_dy = recv_dy.reshape(-1, feature_count)
-    piece_x = lax.all_gather(rows_x, "dp", axis=0, tiled=True)
-    piece_dy = lax.all_gather(rows_dy, "dp", axis=0, tiled=True)
+    piece_x, piece_dy = series_all_advance(rows_x, rows_dy)
     d_gate, d_up, hidden = local_factors(piece_x, piece_dy, w_gate[0], w_up[0], w_down[0])
     term_gate = outer_sum(d_gate, piece_x)
     term_up = outer_sum(d_up, piece_x)

time: 293 us -> 281 us (0.959)
  blocking collectives: 46.6 us -> 0 us
  starting transfers between devices: 0.08 us -> 18.4 us
  waiting for transfers between devices: 193 us -> 210 us
    all_to_all x2 -> x0, blocking collectives: 46.6 us -> none  [the longest x1 27.1 us: local(): lax.all_to_all(sent_x, 'expert', split_axis=0, concat_axis=0, tiled=True)]
    all_to_all x0 -> x2, waiting for transfers between devices: none -> 26 us  [the longest x1 14.1 us: local(): lax.all_to_all(sent_x, 'expert', split_axis=0, concat_axis=0, tiled=True)]
    all_to_all x0 -> x2, starting transfers between devices: none -> 18.4 us  [the longest x1 13 us: local(): lax.all_to_all(sent_dy, 'expert', split_axis=0, concat_axis=0, tiled=True)]
    all_gather x2 -> x1, waiting for transfers between devices: 193 us -> 184 us  [series_all_advance(): lax.all_gather(jnp.concatenate([arr, t0], axis=1), 'dp', axis=0, tiled=True)]
    dot_general x1, matrix products: 2.3 us -> 6.1 us  [local_factors(): lax.dot_general(rows_x, weight_up, contract, preferred_element_type=jnp.f...]
    dot_general x3, matrix products: 9.65 us -> 6.47 us  [outer_sum(): lax.dot_general(factor, rows, (((0,), (0,)), ((), ())), preferred_element...]
    dot_general x1, matrix products: 5.53 us -> 2.36 us  [local_factors(): lax.dot_general(rows_dy, weight_down, contract, preferred_element_type=jn...]
  transfers between devices with their start and end apart: 2 -> 3, of which waited for: 2 -> 3; matrix products, arithmetic and copies ran while one was open for 4% -> 1% of each run, Pallas kernels for 0% -> 0%
where the time goes in v1:
time: 281 us; the launch traced here: 280 us
  waiting for transfers between devices  210 us (75%)
  matrix products  22.2 us (8%)
  starting transfers between devices  18.4 us (7%)
  between operations  14.2 us (5%)
  other arithmetic  12.1 us (4%)
  local copies, waits for them, and re-layouts  3.76 us (1%)
    all_gather x1, waiting for transfers between devices, series_all_advance(): lax.all_gather(jnp.concatenate([arr, t0], axis=1), 'dp', axis=0, tiled=True)  184 us
    all_to_all x1, waiting for transfers between devices, local(): lax.all_to_all(sent_x, 'expert', split_axis=0, concat_axis=0, tiled=True)  14.1 us
    all_to_all x1, starting transfers between devices, local(): lax.all_to_all(sent_dy, 'expert', split_axis=0, concat_axis=0, tiled=True)  13 us
    all_to_all x1, waiting for transfers between devices, local(): lax.all_to_all(sent_dy, 'expert', split_axis=0, concat_axis=0, tiled=True)  11.9 us
    another operation x3, other arithmetic  9.15 us
    dot_general x3, matrix products, outer_sum(): lax.dot_general(factor, rows, (((0,), (0,)), ((), ())), preferred_element...  6.47 us
    dot_general x1, matrix products, local_factors(): lax.dot_general(rows_x, weight_up, contract, preferred_element_type=jnp.f...  6.1 us
  transfers between devices with their start and end apart: 3, of which 3 were waited for; matrix products, arithmetic and copies ran while one was open for 1% of the time, Pallas kernels for 0%

profile of v1, /device:TPU:1, one launch (start us, length us, event | category | flops | bytes accessed | tf_op | source)
XLA Modules:
  0.0 280.4 jit_solution(6570544431004131802)
XLA Ops:
  7.2 0.0 copy-start
  7.2 0.0 copy-start.2
  7.2 0.9 copy.30
  8.1 0.1 eq.43
  8.2 0.1 eq.39
  8.3 9.0 %reduce-window.6 = s32[32,8,128]{2,1,0:T(8,128)S(1)} reduce-window(s32[32,8,128]{2,1,0:T(8,128)S(1)} %fusion.39, s32[]{:T(128)} %constant.4.clone.1), window={size=1x1x128 pad=0_0x0_0x127_0}, to_apply=%region_0.0 | reduce-window | flops 4161536 | bytes 262148 | tf_op jit(solution)/shard_map/reduce-window
  17.3 0.1 slice.8
  17.4 0.1 copy.32
  17.6 0.1 copy.33
  17.6 0.1 broadcast_add_fusion
  17.8 0.1 reduce_sum.30
  17.9 0.7 add_select_fusion
  18.7 1.2 convert_reduce_fusion
  19.9 0.0 copy-done
  19.9 0.3 fusion.21
  20.2 0.9 reshape.64
  21.1 13.0 %all-to-all-start.1 = ((bf16[32,2,3584]{2,1,0:T(2,128)(2,1)}), bf16[32,2,3584]{2,1,0:T(2,128)(2,1)S(1)}, u32[]{:S(2)}, u32[]{:S(2)}) async-start(bf16[32,2,3584]{2,1,0:T(2,128)(2,1)} %reshape.64), calls=%async_computation.1 | async-start | bytes 917504 | tf_op jit(solution)/shard_map/all_to_all | solution.py:64
  34.1 1.4 convolution_convert_fusion
  35.6 0.9 reshape.62
  36.5 11.9 %all-to-all-done.1 = bf16[32,2,3584]{2,1,0:T(2,128)(2,1)S(1)} async-done(((bf16[32,2,3584]{2,1,0:T(2,128)(2,1)}), bf16[32,2,3584]{2,1,0:T(2,128)(2,1)S(1)}, u32[]{:S(2)}, u32[]{:S(2)}) %all-to-all-start.1) | async-done | bytes 458784 | tf_op jit(solution)/shard_map/all_to_all | solution.py:64
  48.4 5.4 %all-to-all-start = ((bf16[32,2,3584]{2,1,0:T(2,128)(2,1)}), bf16[32,2,3584]{2,1,0:T(2,128)(2,1)S(1)}, u32[]{:S(2)}, u32[]{:S(2)}) async-start(bf16[32,2,3584]{2,1,0:T(2,128)(2,1)} %reshape.62), calls=%async_computation | async-start | bytes 917504 | tf_op jit(solution)/shard_map/all_to_all | solution.py:63
  53.8 0.0 all-gather.2.cloned.1.call-start
  53.9 0.2 reshape.65
  54.1 0.0 copy-start.3
  54.1 14.1 %all-to-all-done = bf16[32,2,3584]{2,1,0:T(2,128)(2,1)S(1)} async-done(((bf16[32,2,3584]{2,1,0:T(2,128)(2,1)}), bf16[32,2,3584]{2,1,0:T(2,128)(2,1)S(1)}, u32[]{:S(2)}, u32[]{:S(2)}) %all-to-all-start) | async-done | bytes 458784 | tf_op jit(solution)/shard_map/all_to_all | solution.py:63
  68.1 0.2 reshape.63
  68.3 1.0 pad_maximum_fusion
  69.3 0.0 all-gather.2.cloned.1.call-update
  69.3 183.7 %all-gather.2.cloned.1.call-done = bf16[1024,7168]{1,0:T(8,128)(2,1)} async-done(((bf16[64,7168]{1,0:T(8,128)(2,1)}), bf16[1024,7168]{1,0:T(8,128)(2,1)}) %all-gather.2.cloned.1.call-update) | async-done | bytes 14680080 | tf_op jit(solution)/shard_map/all_gather | solution.py:34
  253.1 0.0 copy-done.2
  253.1 0.0 copy-start.1
  253.1 5.5 %fusion.8 = f32[1024,64]{0,1:T(8,128)S(1)} fusion(bf16[1024,7168]{1,0:T(8,128)(2,1)} %all-gather.2.cloned.1.call-done, bf16[1,64,3584]{2,1,0:T(8,128)(2,1)S(1)} %copy-done.2), kind=kOutput, calls=%fused_computation.8 | convolution fusion | flops 469762048 | bytes 8060928 | tf_op jit(solution)/shard_map/dot_general | solution.py:11
  258.6 0.0 copy-done.3
  258.6 0.0 copy-start.4
  258.6 6.1 %fusion.10 = f32[1024,64]{0,1:T(8,128)S(1)} fusion(bf16[1024,7168]{1,0:T(8,128)(2,1)} %all-gather.2.cloned.1.call-done, bf16[1,64,3584]{2,1,0:T(8,128)(2,1)S(1)} %copy-done.3), kind=kOutput, calls=%fused_computation.10 | convolution fusion | flops 469762048 | bytes 8060928 | tf_op jit(solution)/shard_map/dot_general | solution.py:12
  264.7 0.0 copy-done.1
  264.8 0.0 copy-done.4
  264.8 2.4 fusion.2
  267.1 2.2 fusion.25
  269.3 2.2 fusion.28
  271.4 2.1 fusion.22
  (5 shorter events, 0.1 us)
Async XLA Ops:
  7.2 12.7 %copy-start = (bf16[128,3584]{1,0:T(8,128)(2,1)S(1)}, bf16[128,3584]{1,0:T(8,128)(2,1)}, u32[]{:S(2)}) copy-start(bf16[128,3584]{1,0:T(8,128)(2,1)} %param.10) | copy-start | bytes 2752516
  7.2 245.9 %copy-start.2 = (bf16[1,64,3584]{2,1,0:T(8,128)(2,1)S(1)}, bf16[1,64,3584]{2,1,0:T(8,128)(2,1)}, u32[]{:S(2)}) copy-start(bf16[1,64,3584]{2,1,0:T(8,128)(2,1)} %param.11) | copy-start | bytes 1376260
  21.1 27.3 %all-to-all-start.1 = ((bf16[32,2,3584]{2,1,0:T(2,128)(2,1)}), bf16[32,2,3584]{2,1,0:T(2,128)(2,1)S(1)}, u32[]{:S(2)}, u32[]{:S(2)}) async-start(bf16[32,2,3584]{2,1,0:T(2,128)(2,1)} %reshape.64), calls=%async_computation.1 | async-start | bytes 917504 | tf_op jit(solution)/shard_map/all_to_all | solution.py:64
  48.4 19.7 %all-to-all-start = ((bf16[32,2,3584]{2,1,0:T(2,128)(2,1)}), bf16[32,2,3584]{2,1,0:T(2,128)(2,1)S(1)}, u32[]{:S(2)}, u32[]{:S(2)}) async-start(bf16[32,2,3584]{2,1,0:T(2,128)(2,1)} %reshape.62), calls=%async_computation | async-start | bytes 917504 | tf_op jit(solution)/shard_map/all_to_all | solution.py:63
  53.8 199.2 %all-gather.2.cloned.1.call-start = ((), (), s32[]{:S(2)}) async-start(), calls=%async_computation.2 | async-start | bytes 15597568 | tf_op jit(solution)/shard_map/all_gather | solution.py:34
  54.1 204.5 %copy-start.3 = (bf16[1,64,3584]{2,1,0:T(8,128)(2,1)S(1)}, bf16[1,64,3584]{2,1,0:T(8,128)(2,1)}, u32[]{:S(2)}) copy-start(bf16[1,64,3584]{2,1,0:T(8,128)(2,1)} %param.12) | copy-start | bytes 1376260
  253.1 11.7 %copy-start.1 = (bf16[1024,7168]{1,0:T(8,128)(2,1)S(1)}, bf16[1024,7168]{1,0:T(8,128)(2,1)}, u32[]{:S(2)}) copy-start(bf16[1024,7168]{1,0:T(8,128)(2,1)} %all-gather.2.cloned.1.call-done) | copy-start | bytes 44040196
  258.6 6.1 %copy-start.4 = (bf16[1,64,3584]{2,1,0:T(8,128)(2,1)S(1)}, bf16[1,64,3584]{2,1,0:T(8,128)(2,1)}, u32[]{:S(2)}) copy-start(bf16[1,64,3584]{2,1,0:T(8,128)(2,1)} %param.13) | copy-start | bytes 1376260
Sparse Core Ops, SparseCore 0:
  69.4 183.5 all-gather.1
